TPU v7x, 32 devices: a whole 2x2x4 slice. The times are simulated.
32 devices in a mesh: dp: 4 (over y, x), ctx: 8 (over z, core).
Axes of the slice: x: 2, y: 2, z: 4, core: 2. Of those that a mesh axis runs over, the one named last changes fastest.
Arguments:
- tokens: bfloat16 [4096, 2048], P('ctx', 'dp'), may hold values from -6 to 6
- input_gain: float32 [2048], replicated, may hold values from 0.1 to 1.9
- projections: bfloat16 [3, 2048, 1024], P(None, 'dp'), may hold values from -0.125 to 0.125
- head_gain: float32 [1024], P('dp'), may hold values from 0.1 to 1.9
Outputs:
- attended: bfloat16 [4096, 1024], P('ctx', 'dp')
All inputs are finite; a program needn't handle non-finite values.
Results may differ from a plain program's by a relative error of at most 0.0061.
Values may be sent and summed in bfloat16 or wider, within the bound.
No kernel may reach another device: no remote copies, remote signals or barrier semaphores. Data moves between devices by JAX's collectives and lax.ppermute only.
A program may use at most 64 MiB of HBM per device.

v0:
```python
import jax
import jax.numpy as jnp
from jax import lax
from jax.sharding import PartitionSpec as P

HEAD_DIM = 128
epsilon = 1e-05


def entering(value, axis, join, neutral):
    count, mine = (lax.axis_size(axis), lax.axis_index(axis))
    pieces = lax.all_gather(value, axis)
    subtotal = jnp.full_like(value, 0) + jnp.asarray(neutral, value.dtype)

    def turn(position, subtotal):
        longer = join(subtotal, pieces[position])
        return jnp.where(position < mine, longer, subtotal)

    return lax.fori_loop(0, count - 1, turn, subtotal)


def feature(inputs):
    return jnp.where(inputs > 0, inputs + 1.0, jnp.exp(jnp.minimum(inputs, 0.0)))


def activate(products):
    return jnp.concatenate([feature(products[:2]), products[2:]], axis=0).astype(jnp.bfloat16)


def combine(earlier, later):
    return earlier + later


def body(tokens, input_gain, projections, head_gain):
    whole = lax.all_gather(tokens, "dp", axis=1, tiled=True)
    inputs = whole.astype(jnp.float32)
    steps = inputs.shape[0]
    scale = lax.rsqrt(jnp.mean(inputs * inputs, axis=-1, keepdims=True) + epsilon)
    normed = (inputs * scale * input_gain).astype(jnp.bfloat16)
    width = head_gain.shape[0]
    mine = lax.all_to_all(projections, "dp", split_axis=2, concat_axis=1, tiled=True)
    products = jnp.einsum("td,pdc->ptc", normed, mine, preferred_element_type=jnp.float32)
    stacked = activate(products)
    heads = width // HEAD_DIM
    queries = stacked[0].reshape(steps, heads, HEAD_DIM)
    key_feats = stacked[1].reshape(steps, heads, HEAD_DIM)
    values = stacked[2].reshape(steps, heads, HEAD_DIM)
    local_state = jnp.einsum("the,thf->hef", key_feats, values, preferred_element_type=jnp.float32)
    prior = entering(local_state, "ctx", combine, jnp.zeros_like(local_state))
    prior_state = prior.astype(jnp.bfloat16)
    positions = jnp.arange(steps, dtype=jnp.int32)
    causal = positions[:, None] >= positions[None, :]
    scores = jnp.einsum("the,she->hts", queries, key_feats, preferred_element_type=jnp.float32)
    scores = jnp.where(causal[None], scores, 0.0).astype(jnp.bfloat16)
    inner = jnp.einsum("hts,shf->thf", scores, values, preferred_element_type=jnp.float32)
    outer = jnp.einsum("the,hef->thf", queries, prior_state, preferred_element_type=jnp.float32)
    mixed_out = inner + outer
    factor = lax.rsqrt(jnp.mean(mixed_out * mixed_out, axis=-1, keepdims=True) + epsilon)
    attended = mixed_out * factor * head_gain.reshape(heads, HEAD_DIM)
    return attended.astype(jnp.bfloat16).reshape(steps, width)


def solution(mesh):
    in_specs = (P("ctx", "dp"), P(), P(None, "dp", None), P("dp"))
    out_specs = P("ctx", "dp")
    return jax.shard_map(body, mesh=mesh, in_specs=in_specs, out_specs=out_specs, check_vma=False)
```

profile of v0, /device:TPU:0, one launch (start us, length us, event | category | flops | bytes accessed | tf_op | source)
XLA Modules:
  0.0 136.9 jit_solution(17386029378452002127)
XLA Ops:
  6.5 0.0 all-gather.4.cloned.1.call-start
  6.5 0.7 all-gather.4.cloned.1.call-update
  7.3 0.0 all-gather.6.cloned.1.call-start
  7.3 7.6 %copy.10 = bf16[3,512,1024]{1,0,2:T(4,128)(2,1)} copy(bf16[3,512,1024]{2,1,0:T(8,128)(2,1)} %param.8) | data formatting | bytes 6291456 | tf_op args[2]
  14.9 69.5 %all_to_all.18 = bf16[3,512,1024]{1,0,2:T(4,128)(2,1)S(1)} all-to-all(bf16[3,512,1024]{1,0,2:T(4,128)(2,1)} %copy.10), channel_id=1, replica_groups=mesh['dp'=4,'ctx'=8] {'dp'}, dimensions={2} | all-to-all | bytes 6291456 | tf_op jit(solution)/shard_map/all_to_all | solution.py:41
  84.4 3.0 %copy.20 = bf16[3,512,4,256]{1,2,3,0:T(4,128)(2,1)S(1)} copy(bf16[3,512,4,256]{1,0,3,2:T(4,128)(2,1)S(1)} %bitcast.32) | data formatting | bytes 6291456 | tf_op jit(solution)/shard_map/all_to_all | solution.py:41
  87.4 0.0 copy-start.1
  87.4 4.0 %all_to_all.16 = bf16[3,2048,256]{1,2,0:T(8,128)(2,1)} reshape(bf16[3,4,512,256]{2,1,3,0:T(4,128)(2,1)S(1)} %bitcast.33) | data formatting | bytes 6291456 | tf_op jit(solution)/shard_map/all_to_all | solution.py:41
  91.4 0.0 all-gather.4.cloned.1.call-done
  91.4 2.1 %fusion = f32[512]{0:T(512)S(1)} fusion(bf16[512,2048]{1,0:T(8,128)(2,1)} %all-gather.4.cloned.1.call-done), kind=kLoop, calls=%fused_computation.3 | loop fusion | flops 3145216 | bytes 2099200 | tf_op jit(solution)/shard_map/reduce_sum | solution.py:38
  93.5 0.0 copy-done.1
  93.5 4.4 %fusion.8 = f32[3,512,256]{1,2,0:T(8,128)S(1)} fusion(bf16[3,2048,256]{1,2,0:T(8,128)(2,1)} %all_to_all.16, bf16[512,2048]{1,0:T(8,128)(2,1)} %all-gather.4.cloned.1.call-done, f32[2048]{0:T(1024)S(1)} %copy-done.1, f32[512]{0:T(512)S(1)} %add_rsqrt_fusion.1), kind=kOutput, calls=%fused_computation.12 | convolution fusion | flops 1614807040 | bytes 6825984 | tf_op jit(solution)/shard_map/td,pdc->ptc/dot_general | solution.py:42
  97.9 0.2 select_convert_fusion.1
  98.2 0.9 fusion.20
  99.1 0.0 copy-start
  99.1 0.0 all-gather.6.cloned.1.call-update
  99.1 0.1 iota_compare_fusion
  99.2 22.0 %all-gather.6.cloned.1.call-done = f32[16,128,128]{2,1,0:T(8,128)} async-done(((f32[2,128,128]{2,1,0:T(8,128)}), f32[16,128,128]{2,1,0:T(8,128)}) %all-gather.6.cloned.1.call-update) | async-done | bytes 1048592 | tf_op jit(solution)/shard_map/all_gather | solution.py:12
  121.3 6.8 %while.14 = (s32[]{:T(128)}, f32[2,128,128]{2,1,0:T(8,128)S(1)}, s32[]{:T(128)}, f32[8,2,128,128]{3,2,1,0:T(8,128)}, s32[]{:T(128)}, /*index=5*/s32[]{:T(128)}) while((s32[]{:T(128)}, f32[2,128,128]{2,1,0:T(8,128)S(1)}, s32[]{:T(128)}, f32[8,2,128,128]{3,2,1,0:T(8,128)}, s32[]{:T(128)}, /*index=5*/s32[]{:T(128)}) %tuple.41), condition=%wide.region_2.3_spmd.clone, body=%wide.region_1.2_spmd.clone.sunk | while | flops 98308 | bytes 393317 | solution.py:19
  121.3 0.9 add_select_fusion.2
  122.2 0.9 add_select_fusion.2
  123.2 0.9 add_select_fusion.2
  124.2 0.9 add_select_fusion.2
  125.1 0.9 add_select_fusion.2
  126.1 0.9 add_select_fusion.2
  127.1 0.9 add_select_fusion.2
  128.1 0.3 fusion.16
  128.3 0.8 multiply_reduce_fusion
  129.1 0.0 copy-done
  129.2 0.1 multiply_convert_fusion
  129.3 0.8 copy.15
  (5 shorter events, 0.1 us)
Async XLA Ops:
  6.5 84.8 %all-gather.4.cloned.1.call-start = ((), (), s32[]{:S(2)}) async-start(), calls=%async_computation.1 | async-start | bytes 2621440 | tf_op jit(solution)/shard_map/all_gather | solution.py:35
  7.3 114.0 %all-gather.6.cloned.1.call-start = ((), (), s32[]{:S(2)}) async-start(), calls=%async_computation.2 | async-start | bytes 1179648 | tf_op jit(solution)/shard_map/all_gather | solution.py:12
  87.4 6.1 %copy-start.1 = (f32[2048]{0:T(1024)S(1)}, f32[2048]{0:T(1024)}, u32[]{:S(2)}) copy-start(f32[2048]{0:T(1024)} %param.7) | copy-start | bytes 24580
  99.1 30.0 %copy-start = (f32[256]{0:T(256)S(1)}, f32[256]{0:T(256)}, u32[]{:S(2)}) copy-start(f32[256]{0:T(256)} %param.9) | copy-start | bytes 3076
Sparse Core Ops, SparseCore 0:
  9.2 70.0 all-gather.3
  99.3 21.9 all-gather.5
where the time goes:
time: 137 us
  blocking collectives  69.5 us (51%)
  waiting for transfers between devices  22.7 us (17%)
  local copies, waits for them, and re-layouts  15.5 us (11%)
  between operations  13.5 us (10%)
  other arithmetic  9.16 us (7%)
  matrix products  6.37 us (5%)
    all_to_all x1, blocking collectives, body(): lax.all_to_all(projections, 'dp', split_axis=2, concat_axis=1, tiled=True)  69.5 us
    all_gather x1, waiting for transfers between devices, entering(): pieces = lax.all_gather(value, axis)  22 us
    unnamed x5, local copies, waits for them, and re-layouts  7.62 us
    all_to_all x2, local copies, waits for them, and re-layouts, body(): lax.all_to_all(projections, 'dp', split_axis=2, concat_axis=1, tiled=True)  6.93 us
    select_n x7, other arithmetic, turn(): return jnp.where(position < mine, longer, subtotal)  6.65 us
    dot_general x1, matrix products, body(): jnp.einsum('td,pdc->ptc', normed, mine, preferred_element_type=jnp.float32)  4.42 us
  transfers between devices with their start and end apart: 2, of which 1 were waited for; matrix products, arithmetic and copies ran while one was open for 8% of the time, Pallas kernels for 0%

commit v1 on v0

--- a/solution.py
+++ b/solution.py
@@ -5,6 +5,15 @@
 
 HEAD_DIM = 128
 epsilon = 1e-05
+
+
+def show_cycles(here_x, which_axis, ndim_at, where_dim):
+    return jnp.concatenate(
+        lax.all_to_all(
+            jnp.stack(jnp.split(here_x, lax.axis_size(which_axis), ndim_at), 0), which_axis, 0, 0
+        ),
+        where_dim,
+    )
 
 
 def entering(value, axis, join, neutral):
@@ -38,7 +47,7 @@
     scale = lax.rsqrt(jnp.mean(inputs * inputs, axis=-1, keepdims=True) + epsilon)
     normed = (inputs * scale * input_gain).astype(jnp.bfloat16)
     width = head_gain.shape[0]
-    mine = lax.all_to_all(projections, "dp", split_axis=2, concat_axis=1, tiled=True)
+    mine = show_cycles(projections, "dp", 2, 1)
     products = jnp.einsum("td,pdc->ptc", normed, mine, preferred_element_type=jnp.float32)
     stacked = activate(products)
     heads = width // HEAD_DIM

time: 137 us -> 122 us (0.89)
  blocking collectives: 69.5 us -> 57.6 us
  local copies, waits for them, and re-layouts: 15.5 us -> 12.1 us
    all_to_all x1, blocking collectives: 69.5 us -> 57.6 us  [show_cycles(): lax.all_to_all(jnp.stack(jnp.split(here_x, lax.axis_size(which_axis), ndi...]
    reshape x0 -> x2, local copies, waits for them, and re-layouts: none -> 9.09 us  [show_cycles(): jnp.concatenate(lax.all_to_all(jnp.stack(jnp.split(here_x, lax.axis_size(...]
    unnamed x5 -> x4, local copies, waits for them, and re-layouts: 7.62 us -> 0.01 us
    all_to_all x2 -> x0, local copies, waits for them, and re-layouts: 6.93 us -> none  [body(): lax.all_to_all(projections, 'dp', split_axis=2, concat_axis=1, tiled=True)]
    another operation x0 -> x1, local copies, waits for them, and re-layouts: none -> 2.09 us  [show_cycles(): jnp.stack(jnp.split(here_x, lax.axis_size(which_axis), ndim_at), 0)]
  transfers between devices with their start and end apart: 2 -> 2, of which waited for: 1 -> 1; matrix products, arithmetic and copies ran while one was open for 8% -> 10% of each run, Pallas kernels for 0% -> 0%
where the time goes in v1:
time: 122 us
  blocking collectives  57.6 us (47%)
  waiting for transfers between devices  23.6 us (19%)
  between operations  13.5 us (11%)
  local copies, waits for them, and re-layouts  12.1 us (10%)
  other arithmetic  9.6 us (8%)
  matrix products  5.44 us (4%)
    all_to_all x1, blocking collectives, show_cycles(): lax.all_to_all(jnp.stack(jnp.split(here_x, lax.axis_size(which_axis), ndi...  57.6 us
    all_gather x1, waiting for transfers between devices, entering(): pieces = lax.all_gather(value, axis)  22.8 us
    reshape x2, local copies, waits for them, and re-layouts, show_cycles(): jnp.concatenate(lax.all_to_all(jnp.stack(jnp.split(here_x, lax.axis_size(...  9.09 us
    select_n x7, other arithmetic, turn(): return jnp.where(position < mine, longer, subtotal)  6.65 us
    dot_general x1, matrix products, body(): jnp.einsum('td,pdc->ptc', normed, mine, preferred_element_type=jnp.float32)  3.49 us
  transfers between devices with their start and end apart: 2, of which 1 were waited for; matrix products, arithmetic and copies ran while one was open for 10% of the time, Pallas kernels for 0%

profile of v1, /device:TPU:0, one launch (start us, length us, event | category | flops | bytes accessed | tf_op | source)
XLA Modules:
  0.0 122.0 jit_solution(5105363286985591891)
XLA Ops:
  6.5 0.0 all-gather.4.cloned.1.call-start
  6.5 0.7 all-gather.4.cloned.1.call-update
  7.3 0.0 all-gather.6.cloned.1.call-start
  7.3 2.1 %slice_bitcast_fusion.3 = (bf16[1,3,512,256]{3,2,1,0:T(8,128)(2,1)S(1)}, bf16[1,3,512,256]{3,2,1,0:T(8,128)(2,1)S(1)}, bf16[1,3,512,256]{3,2,1,0:T(8,128)(2,1)S(1)}, bf16[1,3,512,256]{3,2,1,0:T(8,128)(2,1)S(1)}) fusion(bf16[3,512,1024]{2,1,0:T(8,128)(2,1)} %param.8), kind=kLoop, calls=%fused_computation.23 | loop fusion | bytes 6291456 | tf_op jit(solution)/shard_map/stack | solution.py:13
  9.4 0.4 pad_maximum_fusion
  9.8 57.6 %all_to_all.5 = bf16[4,3,512,256]{3,2,1,0:T(8,128)(2,1)S(1)} all-to-all(bf16[4,3,512,256]{3,2,1,0:T(8,128)(2,1)S(1)} %pad_maximum_fusion), channel_id=1, replica_groups=mesh['dp'=4,'ctx'=8] {'dp'}, dimensions={0} | all-to-all | bytes 6291456 | tf_op jit(solution)/shard_map/all_to_all | solution.py:12
  67.4 4.4 %copy.10 = bf16[3,4,512,256]{2,1,3,0:T(4,128)(2,1)} copy(bf16[3,4,512,256]{3,2,0,1:T(8,128)(2,1)S(1)} %bitcast.37) | data formatting | bytes 6291456 | tf_op jit(solution)/shard_map/reshape | solution.py:11
  71.8 0.0 copy-start.1
  71.8 4.7 %reshape.40 = bf16[3,2048,256]{1,2,0:T(8,128)(2,1)S(1)} reshape(bf16[3,4,512,256]{2,1,3,0:T(4,128)(2,1)} %copy.10) | data formatting | bytes 6291456 | tf_op jit(solution)/shard_map/reshape | solution.py:11
  76.5 0.0 all-gather.4.cloned.1.call-done
  76.5 2.1 %fusion = f32[512]{0:T(512)S(1)} fusion(bf16[512,2048]{1,0:T(8,128)(2,1)} %all-gather.4.cloned.1.call-done), kind=kLoop, calls=%fused_computation.3 | loop fusion | flops 3145216 | bytes 2099200 | tf_op jit(solution)/shard_map/reduce_sum | solution.py:47
  78.6 0.0 copy-done.1
  78.6 3.5 %fusion.8 = f32[3,512,256]{1,2,0:T(8,128)S(1)} fusion(bf16[3,2048,256]{1,2,0:T(8,128)(2,1)S(1)} %reshape.40, bf16[512,2048]{1,0:T(8,128)(2,1)} %all-gather.4.cloned.1.call-done, f32[2048]{0:T(1024)S(1)} %copy-done.1, f32[512]{0:T(512)S(1)} %add_rsqrt_fusion.1), kind=kOutput, calls=%fused_computation.12 | convolution fusion | flops 1614807040 | bytes 6825984 | tf_op jit(solution)/shard_map/td,pdc->ptc/dot_general | solution.py:51
  82.1 0.2 select_convert_fusion.1
  82.4 0.9 fusion.20
  83.3 0.0 copy-start
  83.3 0.0 all-gather.6.cloned.1.call-update
  83.4 0.1 iota_compare_fusion
  83.5 22.8 %all-gather.6.cloned.1.call-done = f32[16,128,128]{2,1,0:T(8,128)} async-done(((f32[2,128,128]{2,1,0:T(8,128)}), f32[16,128,128]{2,1,0:T(8,128)}) %all-gather.6.cloned.1.call-update) | async-done | bytes 1048592 | tf_op jit(solution)/shard_map/all_gather | solution.py:21
  106.3 6.8 %while.14 = (s32[]{:T(128)}, f32[2,128,128]{2,1,0:T(8,128)S(1)}, s32[]{:T(128)}, f32[8,2,128,128]{3,2,1,0:T(8,128)}, s32[]{:T(128)}, /*index=5*/s32[]{:T(128)}) while((s32[]{:T(128)}, f32[2,128,128]{2,1,0:T(8,128)S(1)}, s32[]{:T(128)}, f32[8,2,128,128]{3,2,1,0:T(8,128)}, s32[]{:T(128)}, /*index=5*/s32[]{:T(128)}) %tuple.44), condition=%wide.region_2.3_spmd.clone, body=%wide.region_1.2_spmd.clone.sunk | while | flops 98308 | bytes 393309 | solution.py:28
  106.3 0.9 add_select_fusion.2
  107.3 0.9 add_select_fusion.2
  108.2 0.9 add_select_fusion.2
  109.2 0.9 add_select_fusion.2
  110.2 0.9 add_select_fusion.2
  111.2 0.9 add_select_fusion.2
  112.1 0.9 add_select_fusion.2
  113.1 0.3 fusion.16
  113.4 0.8 multiply_reduce_fusion
  114.2 0.0 copy-done
  114.2 0.1 multiply_convert_fusion
  114.3 0.8 copy.14
  (5 shorter events, 0.1 us)
Async XLA Ops:
  6.5 70.0 %all-gather.4.cloned.1.call-start = ((), (), s32[]{:S(2)}) async-start(), calls=%async_computation.1 | async-start | bytes 2621440 | tf_op jit(solution)/shard_map/all_gather | solution.py:44
  7.3 99.0 %all-gather.6.cloned.1.call-start = ((), (), s32[]{:S(2)}) async-start(), calls=%async_computation.2 | async-start | bytes 1179648 | tf_op jit(solution)/shard_map/all_gather | solution.py:21
  71.8 6.8 %copy-start.1 = (f32[2048]{0:T(1024)S(1)}, f32[2048]{0:T(1024)}, u32[]{:S(2)}) copy-start(f32[2048]{0:T(1024)} %param.7) | copy-start | bytes 24580
  83.3 30.8 %copy-start = (f32[256]{0:T(256)S(1)}, f32[256]{0:T(256)}, u32[]{:S(2)}) copy-start(f32[256]{0:T(256)} %param.9) | copy-start | bytes 3076
Sparse Core Ops, SparseCore 0:
  9.2 58.7 all-gather.3
  83.5 22.7 all-gather.5
